TPU v7x, 32 devices: a whole 2x2x4 slice. The times are simulated.
32 devices in a mesh: track: 4 (over y, x), tm: 8 (over z, core).
Axes of the slice: x: 2, y: 2, z: 4, core: 2. Of those that a mesh axis runs over, the one named last changes fastest.
Arguments:
- observations: float32 [1024, 16, 128], P('tm', 'track'), may hold values from -18 to 18
- dynamics: bfloat16 [256, 128, 128], P('track'), may hold values from -1 to 1
- smoother_gain: bfloat16 [256, 128, 128], P('track'), may hold values from -1 to 1
- gains: bfloat16 [256, 128], P('track'), may hold values from 0 to 1
- regime: int32 [256], P('tm'), may hold values from 0 to 255
Outputs:
- smoothed: float32 [1024, 16, 128], P('tm', 'track')
All inputs are finite; a program needn't handle non-finite values.
Results may differ from a plain program's by a relative error of at most 0.0003.
Values may be sent and summed in bfloat16 or wider, within the bound.
No kernel may reach another device: no remote copies, remote signals or barrier semaphores. Data moves between devices by JAX's collectives and lax.ppermute only.
A program may use at most 64 MiB of HBM per device.

v0:
```python
import jax
import jax.numpy as jnp
import numpy as np
from jax import lax
from jax.sharding import PartitionSpec as P


def prefix(shard, axis, combine, identity, reverse):
    peers, position = (lax.axis_size(axis), lax.axis_index(axis))
    everything = jax.tree.map(lambda part: lax.all_gather(part, axis), shard)
    start = jax.tree.map(
        lambda part, zero: jnp.broadcast_to(jnp.asarray(zero, part.dtype), part.shape),
        shard,
        identity,
    )

    def step(k, before):
        at = peers - 1 - k if reverse else k
        reached = at > position if reverse else at < position
        new = combine(before, jax.tree.map(lambda part: part[at], everything))
        return jax.tree.map(lambda a, b: jnp.where(reached, a, b), new, before)

    return lax.fori_loop(0, peers, step, start)


def from_root(shard, axis, root):
    mine = lax.axis_index(axis) == root
    return lax.psum(jnp.where(mine, shard, jnp.zeros_like(shard)), axis)


def shifted(value, axis, steps):
    count = lax.axis_size(axis)
    initial, last = (max(0, -steps), min(count, count - steps))
    return lax.ppermute(value, axis, [(source, source + steps) for source in range(initial, last)])


def matmul(left, right):
    return jnp.dot(left, right, precision=lax.Precision.HIGHEST)


def compose(earlier, later):
    return (matmul(earlier[0], later[0]), matmul(earlier[1], later[0]) + later[1])


def carried_forward(pair):
    width = pair[0].shape[0]
    identity_pair = (jnp.eye(width, dtype=jnp.float32), jnp.zeros_like(pair[1]))
    return prefix(pair, "tm", compose, identity_pair, False)[1]


def carried_backward(pair):
    width = pair[0].shape[0]
    identity_pair = (jnp.eye(width, dtype=jnp.float32), jnp.zeros_like(pair[1]))
    return prefix(pair, "tm", compose, identity_pair, True)[1]


def spread_forward(pair):
    width = pair[0].shape[0]
    identity_pair = (jnp.eye(width, dtype=jnp.float32), jnp.zeros_like(pair[1]))
    within = prefix(pair, "track", compose, identity_pair, False)
    through = compose(within, pair)
    joined = jnp.concatenate([through[0], through[1]], axis=0)
    total = from_root(joined, "track", lax.axis_size("track") - 1)
    earlier = carried_forward((total[:width], total[width:]))
    return matmul(earlier, within[0]) + within[1]


def spread_backward(pair):
    width = pair[0].shape[0]
    identity_pair = (jnp.eye(width, dtype=jnp.float32), jnp.zeros_like(pair[1]))
    within = prefix(pair, "track", compose, identity_pair, True)
    through = compose(within, pair)
    joined = jnp.concatenate([through[0], through[1]], axis=0)
    total = from_root(joined, "track", 0)
    later = carried_backward((total[:width], total[width:]))
    return matmul(later, within[0]) + within[1]


def pick_rows(block_ids, dynamics, smoother_gain, gains):
    owned = dynamics.shape[0]
    width = dynamics.shape[1]
    offset = lax.axis_index("track") * owned
    selector = (block_ids[:, None] - offset == jnp.arange(owned, dtype=jnp.int32)[None, :]).astype(
        jnp.bfloat16
    )
    pick_dyn = jnp.dot(
        selector, dynamics.reshape(owned, width * width), preferred_element_type=jnp.float32
    )
    pick_smooth = jnp.dot(
        selector, smoother_gain.reshape(owned, width * width), preferred_element_type=jnp.float32
    )
    pick_gain = jnp.dot(selector, gains, preferred_element_type=jnp.float32)
    return (pick_dyn, pick_smooth, pick_gain)


def local_map(carry, inputs):
    matrix, vector = inputs
    return ((matmul(carry[0], matrix), matmul(carry[1], matrix) + vector), None)


def propagate(state, inputs):
    matrix, vector = inputs
    state = matmul(state, matrix) + vector
    return (state, state)


def retreat(state, inputs):
    matrix, vector = inputs
    state = vector + matmul(state, matrix)
    return (state, state)


def smooth_span(picked, measured, dwell, finishing, forward_carry, backward_carry):
    pick_dyn, pick_smooth, pick_gain = picked
    length, tracks, width = measured.shape
    count = pick_gain.shape[0]
    step_dyn = jnp.repeat(pick_dyn.reshape(count, width, width), dwell, axis=0)
    step_smooth = jnp.repeat(pick_smooth.reshape(count, width, width), dwell, axis=0)
    step_gain = jnp.repeat(pick_gain, dwell, axis=0)[:length]
    current = step_dyn[:length]
    upcoming = step_dyn[1 : length + 1]
    final_row = jnp.arange(length) == length - 1
    live = jnp.where(jnp.logical_and(finishing, final_row), 0.0, 1.0).astype(jnp.float32)
    next_gain = step_smooth[1 : length + 1] * live[:, None, None]
    closed = jnp.swapaxes(current, 1, 2) * (1.0 - step_gain)[:, None, :]
    driven = step_gain[:, None, :] * measured
    empty_vec = jnp.zeros((tracks, width), jnp.float32)
    unit_mat = jnp.eye(width, dtype=jnp.float32)
    filter_pair, _ = lax.scan(local_map, (unit_mat, empty_vec), (closed, driven))
    before = forward_carry(filter_pair)
    _, filtered = lax.scan(propagate, before, (closed, driven))
    cross = jnp.einsum("tij,tjk->tik", next_gain, upcoming, precision=lax.Precision.HIGHEST)
    innovation = filtered - jnp.einsum(
        "tbj,tij->tbi", filtered, cross, precision=lax.Precision.HIGHEST
    )
    gain_rows = jnp.swapaxes(next_gain, 1, 2)
    smooth_pair, _ = lax.scan(
        local_map, (unit_mat, empty_vec), (gain_rows, innovation), reverse=True
    )
    after = backward_carry(smooth_pair)
    _, smoothed = lax.scan(retreat, after, (gain_rows, innovation), reverse=True)
    return smoothed


def body(observations, dynamics, smoother_gain, gains, regime):
    length = observations.shape[0]
    blocks = regime.shape[0]
    dwell = length // blocks
    following = shifted(regime[:1], "tm", -1)
    block_ids = jnp.concatenate([regime, following])
    on_last = lax.axis_index("tm") == lax.axis_size("tm") - 1
    groups = lax.axis_size("track")
    share = blocks // groups
    place = lax.axis_index("track")
    order = (np.arange(groups)[:, None] * share + np.arange(share + 1)[None, :]).reshape(-1)
    spread_ids = block_ids[order]
    picked = pick_rows(spread_ids, dynamics, smoother_gain, gains)
    picked = (
        lax.psum_scatter(
            picked[0].astype(jnp.bfloat16), "track", scatter_dimension=0, tiled=True
        ).astype(jnp.float32),
        lax.psum_scatter(
            picked[1].astype(jnp.bfloat16), "track", scatter_dimension=0, tiled=True
        ).astype(jnp.float32),
        lax.psum_scatter(
            picked[2].astype(jnp.bfloat16), "track", scatter_dimension=0, tiled=True
        ).astype(jnp.float32),
    )
    measured = lax.all_to_all(observations, "track", split_axis=0, concat_axis=1, tiled=True)
    finishing = jnp.logical_and(on_last, place == groups - 1)
    smoothed = smooth_span(picked, measured, dwell, finishing, spread_forward, spread_backward)
    return lax.all_to_all(smoothed, "track", split_axis=1, concat_axis=0, tiled=True)


def solution(mesh):
    placed = (
        P("tm", "track", None),
        P("track", None, None),
        P("track", None, None),
        P("track", None),
        P("tm"),
    )
    return jax.shard_map(
        body, mesh=mesh, in_specs=placed, out_specs=P("tm", "track", None), check_vma=False
    )
```

profile of v0, /device:TPU:0, one launch (start us, length us, event | category | flops | bytes accessed | tf_op | source)
XLA Modules:
  0.0 525.0 jit_solution(3427825557945967753)
XLA Ops:
  6.5 1.4 collective-permute-start
  9.8 1.4 pad_add_fusion
  12.0 4.2 convolution_convert_fusion
  16.2 2.6 convolution_convert_fusion.1
  18.9 5.2 all-to-all-start
  25.6 17.5 %all-reduce.2 = bf16[36,128]{1,0:T(8,128)(2,1)S(1)} all-reduce(bf16[36,128]{1,0:T(8,128)(2,1)S(1)} %convolution_convert_fusion.2), channel_id=12, replica_groups=mesh['track'=4,'tm'=8] {'track'}, use_global_device_ids=true, to_apply=%region_2.0.clone | all-reduce | flops 4608 | bytes 18432
  43.2 58.4 %all-reduce.12.cloned.1.call-done = (bf16[36,16384]{1,0:T(8,128)(2,1)}, bf16[36,16384]{1,0:T(8,128)(2,1)}) async-done(((bf16[36,16384]{1,0:T(8,128)(2,1)}, bf16[36,16384]{1,0:T(8,128)(2,1)}), (bf16[36,16384]{1,0:T(8,128)(2,1)}, bf16[36,16384]{1,0:T(8,128)(2,1)})) %all-reduce.12.cloned.1.call-update) | async-done | bytes 2359312
  101.5 1.6 dynamic-slice_convert_fusion
  104.0 1.3 copy.21
  105.3 1.5 bitcast_multiply_fusion
  106.8 70.1 %while.124 = (s32[]{:T(128)}, f32[128,128]{0,1:T(8,128)S(1)}, f32[16,128]{1,0:T(8,128)S(1)}, f32[32,128,128]{2,1,0:T(8,128)}, f32[32,16,128]{2,1,0:T(8,128)S(1)}, /*index=5*/s32[]{:T(128)}, s32[]{:T(128)}) while((s32[]{:T(128)}, f32[128,128]{0,1:T(8,128)S(1)}, f32[16,128]{1,0:T(8,128)S(1)}, f32[32,128,128]{2,1,0:T(8,128)}, ...), condition=%wide.region_4.5_spmd.clone, body=%wide.region_3.4_spmd.clone.sunk | while | flops 28315648 | bytes 435799 | solution.py:129
  177.0 10.0 %all-gather = f32[512,128]{0,1:T(8,128)S(1)} all-gather(f32[128,128]{0,1:T(8,128)S(1)} %get-tuple-element.758), channel_id=2, replica_groups=mesh['track'=4,'tm'=8] {'track'}, dimensions={0}, use_global_device_ids=true | all-gather | bytes 327680 | tf_op jit(solution)/shard_map/all_gather | solution.py:10
  187.1 7.2 %all-gather.1 = f32[64,128]{1,0:T(8,128)S(1)} all-gather(f32[16,128]{1,0:T(8,128)S(1)} %get-tuple-element.759), channel_id=3, replica_groups=mesh['track'=4,'tm'=8] {'track'}, dimensions={0}, use_global_device_ids=true | all-gather | bytes 40960 | tf_op jit(solution)/shard_map/all_gather | solution.py:10
  194.3 2.1 while.125
  199.0 3.6 fusion.78
  202.6 1.5 fusion.80
  204.1 34.3 %all-reduce.8.cloned.1.call-done = f32[144,128]{1,0:T(8,128)} async-done(((f32[144,128]{1,0:T(8,128)}), f32[144,128]{1,0:T(8,128)}) %all-reduce.8.cloned.1.call-update) | async-done | bytes 73744 | tf_op jit(solution)/shard_map/psum | solution.py:28
  239.3 14.7 %all-gather.2 = f32[1024,128]{1,0:T(8,128)S(1)} all-gather(f32[128,128]{1,0:T(8,128)S(1)} %slice.58), channel_id=4, replica_groups=mesh['track'=4,'tm'=8] {'tm'}, dimensions={0}, use_global_device_ids=true | all-gather | bytes 589824 | tf_op jit(solution)/shard_map/all_gather | solution.py:10
  254.7 14.3 %all-gather.3 = f32[128,128]{1,0:T(8,128)S(1)} all-gather(f32[16,128]{1,0:T(8,128)S(1)} %slice.59), channel_id=5, replica_groups=mesh['track'=4,'tm'=8] {'tm'}, dimensions={0}, use_global_device_ids=true | all-gather | bytes 73728 | tf_op jit(solution)/shard_map/all_gather | solution.py:10
  269.0 1.5 while.126
  270.7 32.9 %while.122 = (s32[]{:T(128)}, f32[16,128]{1,0:T(8,128)S(1)}, f32[32,16,128]{2,1,0:T(8,128)S(1)}, f32[32,128,128]{2,1,0:T(8,128)}, f32[32,16,128]{2,1,0:T(8,128)}, /*index=5*/s32[]{:T(128)}) while((s32[]{:T(128)}, f32[16,128]{1,0:T(8,128)S(1)}, f32[32,16,128]{2,1,0:T(8,128)S(1)}, f32[32,128,128]{2,1,0:T(8,128)}, f32[32,16,128]{2,1,0:T(8,128)}, ...), condition=%wide.region_11.12_spmd, body=%wide.region_10.11_spmd.sunk | while | flops 3147778 | bytes 115781 | solution.py:131
  303.6 3.4 convolution_subtract_fusion
  307.0 70.2 %while.127 = (s32[]{:T(128)}, f32[128,128]{0,1:T(8,128)S(1)}, f32[16,128]{1,0:T(8,128)S(1)}, f32[32,128,128]{2,1,0:T(8,128)}, f32[32,16,128]{2,1,0:T(8,128)S(1)}, /*index=5*/s32[]{:T(128)}, s32[]{:T(128)}, s32[]{:T(128)}) while((s32[]{:T(128)}, f32[128,128]{0,1:T(8,128)S(1)}, f32[16,128]{1,0:T(8,128)S(1)}, ...), condition=%wide.region_13.14_spmd.clone, body=%wide.region_12.13_spmd.clone.sunk | while | flops 28315652 | bytes 435822 | solution.py:137
  377.2 10.7 %all-gather.4 = f32[512,128]{0,1:T(8,128)S(1)} all-gather(f32[128,128]{0,1:T(8,128)S(1)} %get-tuple-element.764), channel_id=6, replica_groups=mesh['track'=4,'tm'=8] {'track'}, dimensions={0}, use_global_device_ids=true | all-gather | bytes 327680 | tf_op jit(solution)/shard_map/all_gather | solution.py:10
  388.1 8.1 %all-gather.5 = f32[64,128]{1,0:T(8,128)S(1)} all-gather(f32[16,128]{1,0:T(8,128)S(1)} %get-tuple-element.765), channel_id=7, replica_groups=mesh['track'=4,'tm'=8] {'track'}, dimensions={0}, use_global_device_ids=true | all-gather | bytes 40960 | tf_op jit(solution)/shard_map/all_gather | solution.py:10
  396.2 2.1 while.128
  399.5 40.9 %all-reduce.10.cloned.1.call-done = f32[144,128]{1,0:T(8,128)} async-done(((f32[144,128]{1,0:T(8,128)}), f32[144,128]{1,0:T(8,128)}) %all-reduce.10.cloned.1.call-update) | async-done | bytes 73744 | tf_op jit(solution)/shard_map/psum | solution.py:28
  441.3 14.7 %all-gather.6 = f32[1024,128]{1,0:T(8,128)S(1)} all-gather(f32[128,128]{1,0:T(8,128)S(1)} %slice.61), channel_id=8, replica_groups=mesh['track'=4,'tm'=8] {'tm'}, dimensions={0}, use_global_device_ids=true | all-gather | bytes 589824 | tf_op jit(solution)/shard_map/all_gather | solution.py:10
  456.7 14.0 %all-gather.7 = f32[128,128]{1,0:T(8,128)S(1)} all-gather(f32[16,128]{1,0:T(8,128)S(1)} %slice.62), channel_id=9, replica_groups=mesh['track'=4,'tm'=8] {'tm'}, dimensions={0}, use_global_device_ids=true | all-gather | bytes 73728 | tf_op jit(solution)/shard_map/all_gather | solution.py:10
  470.7 1.5 while.129
  472.4 35.0 %while.123 = (s32[]{:T(128)}, f32[16,128]{1,0:T(8,128)S(1)}, f32[32,16,128]{2,0,1:T(8,128)S(1)}, f32[32,16,128]{2,1,0:T(8,128)S(1)}, f32[32,128,128]{2,1,0:T(8,128)}, /*index=5*/s32[]{:T(128)}, s32[]{:T(128)}, s32[]{:T(128)}) while((s32[]{:T(128)}, f32[16,128]{1,0:T(8,128)S(1)}, f32[32,16,128]{2,0,1:T(8,128)S(1)}, ...), condition=%wide.region_20.21_spmd, body=%wide.region_19.20_spmd.sunk | while | flops 3147779 | bytes 124005 | solution.py:141
  507.4 10.1 %all_to_all.36 = f32[32,16,128]{2,0,1:T(8,128)S(1)} all-to-all(f32[32,16,128]{2,0,1:T(8,128)S(1)} %get-tuple-element.769), channel_id=1, replica_groups=mesh['track'=4,'tm'=8] {'track'}, dimensions={1} | all-to-all | bytes 524288 | tf_op jit(solution)/shard_map/all_to_all | solution.py:172
  (551 shorter events, 223.7 us)
Async XLA Ops:
  6.5 18.8 %copy-start = (bf16[64,128]{1,0:T(8,128)(2,1)S(1)}, bf16[64,128]{1,0:T(8,128)(2,1)}, u32[]{:S(2)}) copy-start(bf16[64,128]{1,0:T(8,128)(2,1)} %param.26) | copy-start | bytes 49156
  6.5 9.7 %copy-start.6 = (bf16[64,128,128]{2,1,0:T(8,128)(2,1)S(1)}, bf16[64,128,128]{2,1,0:T(8,128)(2,1)}, u32[]{:S(2)}) copy-start(bf16[64,128,128]{2,1,0:T(8,128)(2,1)} %param.25) | copy-start | bytes 6291460
  6.5 95.0 %all-reduce.12.cloned.1.call-start = ((), (), s32[]{:S(2)}) async-start(), calls=%async_computation.4 | async-start | bytes 5242880
  6.5 3.3 collective-permute-start
  18.9 5.3 %copy-start.9 = (u32[32]{0:T(128)S(1)}, u32[32]{0:T(128)}, u32[]{:S(2)}) copy-start(u32[32]{0:T(128)} %constant.255) | copy-start | bytes 388
  18.9 24.2 %all-to-all-start = ((f32[128,4,128]{2,1,0:T(4,128)}), f32[128,4,128]{2,1,0:T(4,128)S(1)}, u32[]{:S(2)}, u32[]{:S(2)}) async-start(f32[128,4,128]{2,1,0:T(4,128)} %param.23), calls=%async_computation | async-start | bytes 524288 | tf_op jit(solution)/shard_map/all_to_all | solution.py:169
  24.1 214.4 %all-reduce.8.cloned.1.call-start = ((), (), s32[]{:S(2)}) async-start(), calls=%async_computation.2 | async-start | bytes 147456 | tf_op jit(solution)/shard_map/psum | solution.py:28
  24.1 79.0 %copy-start.1 = (f32[128,128]{0,1:T(8,128)}, f32[128,128]{0,1:T(8,128)S(1)}, u32[]{:S(2)}) copy-start(f32[128,128]{0,1:T(8,128)S(1)} %fusion.82) | copy-start | bytes 196612
  104.0 2.8 copy-start.3
  106.8 87.5 %copy-start.4 = (f32[128,128]{0,1:T(8,128)S(1)}, f32[128,128]{0,1:T(8,128)}, u32[]{:S(2)}) copy-start(f32[128,128]{0,1:T(8,128)} %copy-done.1) | copy-start | bytes 196612
  176.9 20.7 %copy-start.7 = (f32[32,16,128]{2,1,0:T(8,128)}, f32[32,16,128]{2,1,0:T(8,128)S(1)}, u32[]{:S(2)}) copy-start(f32[32,16,128]{2,1,0:T(8,128)S(1)} %get-tuple-element.1440) | copy-start | bytes 786436
  197.6 242.8 %all-reduce.10.cloned.1.call-start = ((), (), s32[]{:S(2)}) async-start(), calls=%async_computation.3 | async-start | bytes 147456 | tf_op jit(solution)/shard_map/psum | solution.py:28
  202.6 68.1 %copy-start.8 = (f32[32,16,128]{2,1,0:T(8,128)S(1)}, f32[32,16,128]{2,1,0:T(8,128)}, u32[]{:S(2)}) copy-start(f32[32,16,128]{2,1,0:T(8,128)} %custom-call.8) | copy-start | bytes 786436
  254.7 52.2 %copy-start.5 = (f32[128,128]{0,1:T(8,128)S(1)}, f32[128,128]{0,1:T(8,128)}, u32[]{:S(2)}) copy-start(f32[128,128]{0,1:T(8,128)} %copy-done.1) | copy-start | bytes 196612
  307.0 89.2 %copy-start.2 = (f32[128,128]{0,1:T(8,128)S(1)}, f32[128,128]{0,1:T(8,128)}, u32[]{:S(2)}) copy-start(f32[128,128]{0,1:T(8,128)} %copy-done.1) | copy-start | bytes 196612
Sparse Core Ops, SparseCore 0:
  19.0 82.4 all-reduce.11
  197.7 40.6 all-reduce.7
  399.6 40.7 all-reduce.9
where the time goes:
time: 535 us; the launch traced here: 525 us
  matrix products  223 us (42%)
  waiting for transfers between devices  135 us (25%)
  blocking collectives  121 us (23%)
  between operations  14.1 us (3%)
  local copies, waits for them, and re-layouts  12.8 us (2%)
  other arithmetic  8.16 us (2%)
  starting transfers between devices  6.66 us (1%)
    dot_general x230, matrix products, matmul(): return jnp.dot(left, right, precision=lax.Precision.HIGHEST)  208 us
    all_gather x8, blocking collectives, prefix(): everything = jax.tree.map(lambda part: lax.all_gather(part, axis), shard)  93.8 us
    psum x2, waiting for transfers between devices, from_root(): return lax.psum(jnp.where(mine, shard, jnp.zeros_like(shard)), axis)  75.2 us
    unnamed x4, waiting for transfers between devices  58.4 us
    unnamed x1, blocking collectives  17.5 us
  transfers between devices with their start and end apart: 5, of which 4 were waited for; matrix products, arithmetic and copies ran while one was open for 2% of the time, Pallas kernels for 0%

commit v1 on v0

--- a/solution.py
+++ b/solution.py
@@ -25,7 +25,11 @@
 
 def from_root(shard, axis, root):
     mine = lax.axis_index(axis) == root
-    return lax.psum(jnp.where(mine, shard, jnp.zeros_like(shard)), axis)
+
+    def detail_the_outputs(frame_in, chip_axis):
+        return jnp.sum(jax.lax.all_gather(frame_in, chip_axis), axis=0)
+
+    return detail_the_outputs(jnp.where(mine, shard, jnp.zeros_like(shard)), axis)
 
 
 def shifted(value, axis, steps):

time: 535 us -> 421 us (0.79)
  matrix products: 223 us -> 141 us
  waiting for transfers between devices: 135 us -> 58.4 us
  local copies, waits for them, and re-layouts: 12.8 us -> 41.9 us
  blocking collectives: 121 us -> 140 us
    dot_general x230, matrix products: 208 us -> 127 us  [matmul(): return jnp.dot(left, right, precision=lax.Precision.HIGHEST)]
    psum x2 -> x0, waiting for transfers between devices: 75.2 us -> none  [from_root(): return lax.psum(jnp.where(mine, shard, jnp.zeros_like(shard)), axis)]
    while x224, local copies, waits for them, and re-layouts: 1.96 us -> 31.8 us
    all_gather x0 -> x2, blocking collectives: none -> 17.8 us  [detail_the_outputs(): return jnp.sum(jax.lax.all_gather(frame_in, chip_axis), axis=0)]
    unnamed x4 -> x2, waiting for transfers between devices: 58.4 us -> 57.2 us
  transfers between devices with their start and end apart: 5 -> 3, of which waited for: 4 -> 2; matrix products, arithmetic and copies ran while one was open for 2% -> 1% of each run, Pallas kernels for 0% -> 0%
where the time goes in v1:
time: 421 us; the launch traced here: 414 us
  matrix products  141 us (33%)
  blocking collectives  140 us (33%)
  waiting for transfers between devices  58.4 us (14%)
  local copies, waits for them, and re-layouts  41.9 us (10%)
  between operations  14.5 us (3%)
  other arithmetic  8.46 us (2%)
  starting transfers between devices  6.62 us (2%)
    dot_general x230, matrix products, matmul(): return jnp.dot(left, right, precision=lax.Precision.HIGHEST)  127 us
    all_gather x8, blocking collectives, prefix(): everything = jax.tree.map(lambda part: lax.all_gather(part, axis), shard)  95.5 us
    unnamed x2, waiting for transfers between devices  57.2 us
    while x224, local copies, waits for them, and re-layouts  31.8 us
    all_gather x2, blocking collectives, detail_the_outputs(): return jnp.sum(jax.lax.all_gather(frame_in, chip_axis), axis=0)  17.8 us
    unnamed x1, blocking collectives  17.5 us
    all_to_all x1, blocking collectives, body(): lax.all_to_all(smoothed, 'track', split_axis=1, concat_axis=0, tiled=True)  8.89 us
  transfers between devices with their start and end apart: 3, of which 2 were waited for; matrix products, arithmetic and copies ran while one was open for 1% of the time, Pallas kernels for 0%

profile of v1, /device:TPU:0, one launch (start us, length us, event | category | flops | bytes accessed | tf_op | source)
XLA Modules:
  0.0 413.9 jit_solution(17440477247368876040)
XLA Ops:
  12.0 4.2 %convolution_convert_fusion = bf16[36,16384]{1,0:T(8,128)(2,1)} fusion(bf16[8,8,128,128]{3,2,1,0:T(8,128)(2,1)} %bitcast.264, s32[36]{0:T(128)S(1)} %broadcast_subtract_fusion.1), kind=kOutput, calls=%fused_computation.88 | convolution fusion | flops 76089600 | bytes 3276944 | tf_op jit(solution)/shard_map/dot_general | solution.py:90
  16.2 2.6 convolution_convert_fusion.1
  18.9 5.2 %all-to-all-start = ((f32[128,4,128]{2,1,0:T(4,128)}), f32[128,4,128]{2,1,0:T(4,128)S(1)}, u32[]{:S(2)}, u32[]{:S(2)}) async-start(f32[128,4,128]{2,1,0:T(4,128)} %param.23), calls=%async_computation | async-start | bytes 524288 | tf_op jit(solution)/shard_map/all_to_all | solution.py:173
  26.2 17.5 %all-reduce.2 = bf16[36,128]{1,0:T(8,128)(2,1)S(1)} all-reduce(bf16[36,128]{1,0:T(8,128)(2,1)S(1)} %convolution_convert_fusion.2), channel_id=12, replica_groups=mesh['track'=4,'tm'=8] {'track'}, use_global_device_ids=true, to_apply=%region_2.0.clone | all-reduce | flops 4608 | bytes 18432
  44.4 57.2 %all-reduce.6.cloned.1.call-done = (bf16[36,16384]{1,0:T(8,128)(2,1)}, bf16[36,16384]{1,0:T(8,128)(2,1)}) async-done(((bf16[36,16384]{1,0:T(8,128)(2,1)}, bf16[36,16384]{1,0:T(8,128)(2,1)}), (bf16[36,16384]{1,0:T(8,128)(2,1)}, bf16[36,16384]{1,0:T(8,128)(2,1)})) %all-reduce.6.cloned.1.call-update) | async-done | bytes 2359312
  101.5 2.6 dynamic-slice_convert_fusion
  106.5 57.3 %while.124 = (s32[]{:T(128)}, f32[128,128]{0,1:T(8,128)S(1)}, f32[16,128]{1,0:T(8,128)}, f32[32,128,128]{2,1,0:T(8,128)S(1)}, f32[32,16,128]{2,1,0:T(8,128)S(1)}, /*index=5*/s32[]{:T(128)}, s32[]{:T(128)}) while((s32[]{:T(128)}, f32[128,128]{0,1:T(8,128)S(1)}, f32[16,128]{1,0:T(8,128)}, f32[32,128,128]{2,1,0:T(8,128)S(1)}, ...), condition=%wide.region_4.5_spmd.clone, body=%wide.region_3.4_spmd.clone.sunk | while | flops 28315648 | bytes 435291 | solution.py:133
  164.5 10.6 %all-gather = f32[512,128]{0,1:T(8,128)} all-gather(f32[128,128]{0,1:T(8,128)S(1)} %get-tuple-element.758), channel_id=2, replica_groups=mesh['track'=4,'tm'=8] {'track'}, dimensions={0}, use_global_device_ids=true | all-gather | bytes 327680 | tf_op jit(solution)/shard_map/all_gather | solution.py:10
  176.2 8.6 %all-gather.1 = f32[64,128]{1,0:T(8,128)} all-gather(f32[16,128]{1,0:T(8,128)} %get-tuple-element.759), channel_id=3, replica_groups=mesh['track'=4,'tm'=8] {'track'}, dimensions={0}, use_global_device_ids=true | all-gather | bytes 40960 | tf_op jit(solution)/shard_map/all_gather | solution.py:10
  184.8 9.9 %while.125 = (s32[]{:T(128)}, f32[128,128]{0,1:T(8,128)S(1)}, f32[16,128]{1,0:T(8,128)}, s32[]{:T(128)}, f32[4,128,128]{2,1,0:T(8,128)S(1)}, /*index=5*/f32[4,16,128]{2,1,0:T(8,128)}, s32[]{:T(128)}, s32[]{:T(128)}) while((s32[]{:T(128)}, f32[128,128]{0,1:T(8,128)S(1)}, f32[16,128]{1,0:T(8,128)}, s32[]{:T(128)}, ...), condition=%wide.region_6.7_spmd.clone, body=%wide.region_5.6_spmd.clone.sunk | while | flops 28336132 | bytes 510572 | solution.py:23
  196.0 9.0 %all_gather.60 = f32[4,144,128]{2,1,0:T(8,128)} all-gather(f32[1,144,128]{2,1,0:T(8,128)S(1)} %maximum_select_fusion), channel_id=1, replica_groups=mesh['track'=4,'tm'=8] {'track'}, dimensions={0}, use_global_device_ids=true | all-gather | bytes 368640 | tf_op jit(solution)/shard_map/all_gather | solution.py:30
  206.0 15.8 %all-gather.2 = f32[1024,128]{1,0:T(8,128)} all-gather(f32[128,128]{1,0:T(8,128)S(1)} %slice.58), channel_id=4, replica_groups=mesh['track'=4,'tm'=8] {'tm'}, dimensions={0}, use_global_device_ids=true | all-gather | bytes 589824 | tf_op jit(solution)/shard_map/all_gather | solution.py:10
  221.8 14.2 %all-gather.3 = f32[128,128]{1,0:T(8,128)S(1)} all-gather(f32[16,128]{1,0:T(8,128)S(1)} %slice.59), channel_id=5, replica_groups=mesh['track'=4,'tm'=8] {'tm'}, dimensions={0}, use_global_device_ids=true | all-gather | bytes 73728 | tf_op jit(solution)/shard_map/all_gather | solution.py:10
  235.9 18.5 %while.126 = (s32[]{:T(128)}, f32[16,128]{1,0:T(8,128)}, s32[]{:T(128)}, f32[8,128,128]{2,1,0:T(8,128)}, f32[8,16,128]{2,1,0:T(8,128)S(1)}, /*index=5*/s32[]{:T(128)}, s32[]{:T(128)}) while((s32[]{:T(128)}, f32[16,128]{1,0:T(8,128)}, s32[]{:T(128)}, f32[8,128,128]{2,1,0:T(8,128)}, f32[8,16,128]{2,1,0:T(8,128)S(1)}, ...), condition=%wide.region_9.10_spmd.clone, body=%wide.region_8.9_spmd.clone.sunk | while | flops 3153924 | bytes 117343 | solution.py:23
  236.6 1.6 fusion.158
  238.9 1.6 fusion.158
  241.2 1.6 fusion.158
  243.5 1.6 fusion.158
  245.8 1.6 fusion.158
  248.2 1.6 fusion.158
  255.2 47.1 %while.122 = (s32[]{:T(128)}, f32[16,128]{1,0:T(8,128)S(1)}, f32[32,16,128]{2,1,0:T(8,128)}, f32[32,128,128]{2,1,0:T(8,128)S(1)}, f32[32,16,128]{2,1,0:T(8,128)}, /*index=5*/s32[]{:T(128)}) while((s32[]{:T(128)}, f32[16,128]{1,0:T(8,128)S(1)}, f32[32,16,128]{2,1,0:T(8,128)}, f32[32,128,128]{2,1,0:T(8,128)S(1)}, f32[32,16,128]{2,1,0:T(8,128)}, ...), condition=%wide.region_11.12_spmd, body=%wide.region_10.11_spmd.sunk | while | flops 3147778 | bytes 115781 | solution.py:135
  305.4 3.7 fusion.78
  309.1 3.4 convolution_subtract_fusion
  312.6 16.7 %while.127 = (s32[]{:T(128)}, f32[128,128]{0,1:T(8,128)S(1)}, f32[16,128]{1,0:T(8,128)S(1)}, f32[32,128,128]{2,1,0:T(8,128)S(1)}, f32[32,16,128]{2,1,0:T(8,128)S(1)}, /*index=5*/s32[]{:T(128)}, s32[]{:T(128)}, s32[]{:T(128)}) while((s32[]{:T(128)}, f32[128,128]{0,1:T(8,128)S(1)}, f32[16,128]{1,0:T(8,128)S(1)}, ...), condition=%wide.region_13.14_spmd.clone, body=%wide.region_12.13_spmd.clone.sunk | while | flops 28315652 | bytes 435822 | solution.py:141
  329.2 10.1 %all-gather.4 = f32[512,128]{0,1:T(8,128)S(1)} all-gather(f32[128,128]{0,1:T(8,128)S(1)} %get-tuple-element.764), channel_id=6, replica_groups=mesh['track'=4,'tm'=8] {'track'}, dimensions={0}, use_global_device_ids=true | all-gather | bytes 327680 | tf_op jit(solution)/shard_map/all_gather | solution.py:10
  339.4 7.5 %all-gather.5 = f32[64,128]{1,0:T(8,128)S(1)} all-gather(f32[16,128]{1,0:T(8,128)S(1)} %get-tuple-element.765), channel_id=7, replica_groups=mesh['track'=4,'tm'=8] {'track'}, dimensions={0}, use_global_device_ids=true | all-gather | bytes 40960 | tf_op jit(solution)/shard_map/all_gather | solution.py:10
  346.9 2.1 while.128
  349.6 8.8 %all_gather.69 = f32[4,144,128]{2,1,0:T(8,128)S(1)} all-gather(f32[1,144,128]{2,1,0:T(8,128)S(1)} %maximum_select_fusion.1), channel_id=1, replica_groups=mesh['track'=4,'tm'=8] {'track'}, dimensions={0}, use_global_device_ids=true | all-gather | bytes 368640 | tf_op jit(solution)/shard_map/all_gather | solution.py:30
  358.5 14.9 %all-gather.6 = f32[1024,128]{1,0:T(8,128)S(1)} all-gather(f32[128,128]{1,0:T(8,128)S(1)} %slice.61), channel_id=8, replica_groups=mesh['track'=4,'tm'=8] {'tm'}, dimensions={0}, use_global_device_ids=true | all-gather | bytes 589824 | tf_op jit(solution)/shard_map/all_gather | solution.py:10
  373.4 13.9 %all-gather.7 = f32[128,128]{1,0:T(8,128)S(1)} all-gather(f32[16,128]{1,0:T(8,128)S(1)} %slice.62), channel_id=9, replica_groups=mesh['track'=4,'tm'=8] {'tm'}, dimensions={0}, use_global_device_ids=true | all-gather | bytes 73728 | tf_op jit(solution)/shard_map/all_gather | solution.py:10
  389.1 8.2 %while.123 = (s32[]{:T(128)}, f32[16,128]{1,0:T(8,128)S(1)}, f32[32,16,128]{2,0,1:T(8,128)S(1)}, f32[32,16,128]{2,1,0:T(8,128)S(1)}, f32[32,128,128]{2,1,0:T(8,128)S(1)}, /*index=5*/s32[]{:T(128)}, s32[]{:T(128)}, s32[]{:T(128)}) while((s32[]{:T(128)}, f32[16,128]{1,0:T(8,128)S(1)}, f32[32,16,128]{2,0,1:T(8,128)S(1)}, ...), condition=%wide.region_20.21_spmd, body=%wide.region_19.20_spmd.sunk | while | flops 3147779 | bytes 124005 | solution.py:145
  397.3 8.9 %all_to_all.36 = f32[32,16,128]{2,0,1:T(8,128)S(1)} all-to-all(f32[32,16,128]{2,0,1:T(8,128)S(1)} %get-tuple-element.769), channel_id=1, replica_groups=mesh['track'=4,'tm'=8] {'track'}, dimensions={1} | all-to-all | bytes 524288 | tf_op jit(solution)/shard_map/all_to_all | solution.py:176
  (561 shorter events, 169.1 us)
Async XLA Ops:
  6.5 19.4 %copy-start = (bf16[64,128]{1,0:T(8,128)(2,1)S(1)}, bf16[64,128]{1,0:T(8,128)(2,1)}, u32[]{:S(2)}) copy-start(bf16[64,128]{1,0:T(8,128)(2,1)} %param.26) | copy-start | bytes 49156
  6.5 9.7 %copy-start.6 = (bf16[64,128,128]{2,1,0:T(8,128)(2,1)S(1)}, bf16[64,128,128]{2,1,0:T(8,128)(2,1)}, u32[]{:S(2)}) copy-start(bf16[64,128,128]{2,1,0:T(8,128)(2,1)} %param.25) | copy-start | bytes 6291460
  6.5 95.0 %all-reduce.6.cloned.1.call-start = ((), (), s32[]{:S(2)}) async-start(), calls=%async_computation.2 | async-start | bytes 5242880
  6.5 3.3 collective-permute-start
  18.9 5.3 %copy-start.15 = (u32[32]{0:T(128)S(1)}, u32[32]{0:T(128)}, u32[]{:S(2)}) copy-start(u32[32]{0:T(128)} %constant.255) | copy-start | bytes 388
  18.9 25.4 %all-to-all-start = ((f32[128,4,128]{2,1,0:T(4,128)}), f32[128,4,128]{2,1,0:T(4,128)S(1)}, u32[]{:S(2)}, u32[]{:S(2)}) async-start(f32[128,4,128]{2,1,0:T(4,128)} %param.23), calls=%async_computation | async-start | bytes 524288 | tf_op jit(solution)/shard_map/all_to_all | solution.py:173
  24.1 80.0 %copy-start.1 = (f32[128,128]{0,1:T(8,128)}, f32[128,128]{0,1:T(8,128)S(1)}, u32[]{:S(2)}) copy-start(f32[128,128]{0,1:T(8,128)S(1)} %fusion.84) | copy-start | bytes 196612
  101.5 3.7 copy-start.13
  104.2 2.4 copy-start.3
  106.5 78.3 %copy-start.4 = (f32[128,128]{0,1:T(8,128)S(1)}, f32[128,128]{0,1:T(8,128)}, u32[]{:S(2)}) copy-start(f32[128,128]{0,1:T(8,128)} %copy-done.1) | copy-start | bytes 196612
  163.8 0.7 copy-start.7
  194.7 59.7 %copy-start.10 = (f32[16,128]{1,0:T(8,128)S(1)}, f32[16,128]{1,0:T(8,128)}, u32[]{:S(2)}) copy-start(f32[16,128]{1,0:T(8,128)} %get-tuple-element.761) | copy-start | bytes 24580
  304.3 0.7 copy-start.14
  305.4 3.7 copy-start.12
  309.1 3.4 copy-start.5
  309.1 3.4 copy-start.8
  312.5 34.4 %copy-start.2 = (f32[128,128]{0,1:T(8,128)S(1)}, f32[128,128]{0,1:T(8,128)}, u32[]{:S(2)}) copy-start(f32[128,128]{0,1:T(8,128)} %copy-done.1) | copy-start | bytes 196612
  312.5 34.4 %copy-start.9 = (f32[16,128]{1,0:T(8,128)S(1)}, f32[16,128]{1,0:T(8,128)}, u32[]{:S(2)}) copy-start(f32[16,128]{1,0:T(8,128)} %custom-call.4) | copy-start | bytes 24580
  346.9 40.4 %copy-start.11 = (f32[16,128]{1,0:T(8,128)S(1)}, f32[16,128]{1,0:T(8,128)}, u32[]{:S(2)}) copy-start(f32[16,128]{1,0:T(8,128)} %custom-call.5) | copy-start | bytes 24580
Sparse Core Ops, SparseCore 0:
  19.0 82.4 all-reduce.5
